TPU v7x, 32 devices: a whole 2x2x4 slice. The times are simulated.
32 devices in a mesh: grp: 2 (over y), gx: 4 (over z), gy: 2 (over x), row: 2 (over core).
Axes of the slice: x: 2, y: 2, z: 4, core: 2. Of those that a mesh axis runs over, the one named last changes fastest.
Arguments:
- conc: float32 [64, 8, 16, 128], P(None, ('grp', 'gx'), ('gy', 'row')), parts along dimension 1, may hold values from 0.2 to 2
- cotangent: float32 [64, 8, 16, 128], P(None, ('grp', 'gx'), ('gy', 'row')), parts along dimension 1, may hold values from -6 to 6
- courant: float32 [32, 128], P(('grp', 'gy', 'row')), parts along dimension 0, may hold values from 8 to 100
- direction: int32 [32, 128], P(('grp', 'gy', 'row')), parts along dimension 0, may hold values 0 or 1
- rate_const: float32 [1024], replicated, may hold values from 0.01 to 0.1
- orders: int32 [1024, 64], replicated, may hold values from 0 to 2, as said below
- stoich: int32 [64, 1024], replicated, may hold values from -2 to 1, as said below
Outputs:
- final_state: float32 [64, 8, 16, 128], P(None, ('grp', 'gx'), ('gy', 'row')), parts along dimension 1
- adjoint: float32 [64, 8, 16, 128], P(None, ('grp', 'gx'), ('gy', 'row')), parts along dimension 1
There are 2 independent parts, one for each index of `grp`. A program takes and returns all parts, laid end to end along the dimension named above; an argument that names none is the same for every part. Nothing has to cross between parts.
Inputs may be any that keep to these rules, and one draw needn't show every extreme that they name: `orders`: each reaction has two different reactants, each of order 1 or 2, and no other nonzero order. stoich[s, j] is 1 for the product species of reaction j (one species) minus orders[j, s].
All inputs are finite; a program needn't handle non-finite values. No bound on the sum of `direction` on one device may be relied on, other than what follows from the above.
Results may differ from a plain program's by a relative error of at most 0.0003.
Values sent between devices are 32-bit elements; how exact they have to be, the bound alone decides.
A program may use at most 64 MiB of HBM per device.

v0:
```python
import jax
import jax.numpy as jnp
from jax import lax
from jax.sharding import PartitionSpec as P

STEPS = 2


time_step = 0.1
diffusion = 0.1
highest = lax.Precision.HIGHEST


def padded_2(block, sides, width):
    for axis, dim in sides:
        count = lax.axis_size(axis)
        forward = [(i, i + 1) for i in range(count - 1)]
        backward = [(target, source) for source, target in forward]
        low = lax.ppermute(
            lax.slice_in_dim(block, block.shape[dim] - width, None, axis=dim), axis, forward
        )
        high = lax.ppermute(lax.slice_in_dim(block, 0, width, axis=dim), axis, backward)
        block = jnp.concatenate([low, block, high], axis=dim)
    return block


def combine_pairs(leading, trailing):
    return (leading[0] * trailing[0], trailing[0] * leading[1] + trailing[1])


def recurrence(values, weight, backward):
    multipliers = jnp.broadcast_to(weight[None, None], (1, values.shape[1]) + weight.shape)
    return lax.associative_scan(combine_pairs, (multipliers, values), reverse=backward, axis=1)


def sweep_fields(fields, weight, mask):
    stacked = jnp.stack(fields)
    pencils = lax.all_to_all(stacked, "gx", split_axis=1, concat_axis=2, tiled=True)
    rising = recurrence(pencils[0], weight, False)[1]
    falling = recurrence(pencils[-1], weight, True)[1]
    results = jnp.stack([jnp.where(mask, rising, falling)])
    back = lax.all_to_all(results, "gx", split_axis=2, concat_axis=1, tiled=True)
    return [back[0]]


def sweep(values, weight, upward):
    return sweep_fields([values], weight, upward[None, None])[0]


def smooth_padded(values, padded):
    widths = [(0, 0)] * (padded.ndim - 1) + [(1, 1)]
    padded = jnp.pad(padded, widths)
    beside_all = (
        padded[..., 2:, 1:-1]
        + padded[..., :-2, 1:-1]
        + padded[..., 1:-1, 2:]
        + padded[..., 1:-1, :-2]
    )
    return values + diffusion * (beside_all - 4.0 * values)


def smooth(values):
    padded = padded_2(values, ((("gy", "row"), 2),), 1)
    return smooth_padded(values, padded)


def reaction_rates(cells, order_float, rate_const):
    activity = 0.5 * jnp.log1p(cells * cells)
    return rate_const[:, None] * jnp.exp(jnp.dot(order_float, activity, precision=highest))


def per_slice(function, arrays, shape):
    species, depth = (shape[0], shape[1])
    flats = [item.reshape(species, -1) for item in arrays]
    pieces = function(*[item for item in flats])
    return pieces.reshape(shape)


def shards(conc, cotangent, courant, direction, rate_const, orders, stoich):
    order_float = orders.astype(jnp.float32)
    stoich_float = stoich.astype(jnp.float32)
    order_trans = order_float.T
    stoich_trans = stoich_float.T
    retain = courant / (1.0 + courant)
    admit = 1.0 / (1.0 + courant)

    def react(cells):
        return cells + time_step * jnp.dot(
            stoich_float, reaction_rates(cells, order_float, rate_const), precision=highest
        )

    def react_back(cells, spread):
        rates = reaction_rates(cells, order_float, rate_const)
        pulled = jnp.dot(stoich_trans, spread, precision=highest)
        summed = jnp.dot(order_trans, rates * pulled, precision=highest)
        return spread + time_step * cells / (1.0 + cells * cells) * summed

    upward = direction == 1
    states = [conc]
    for position in range(STEPS):
        current = states[-1]
        starred = per_slice(react, [current], current.shape)
        states.append(sweep(admit * smooth(starred), retain, upward))
    adjoint = cotangent
    for position in reversed(range(STEPS)):
        carried = admit * sweep(adjoint, retain, direction == 0)
        spread = smooth(carried)
        adjoint = per_slice(react_back, [states[position], spread], spread.shape)
    return (states[-1], adjoint)


def solution(mesh):
    placed = (
        P(None, ("grp", "gx"), ("gy", "row"), None),
        P(None, ("grp", "gx"), ("gy", "row"), None),
        P(("grp", "gy", "row"), None),
        P(("grp", "gy", "row"), None),
        P(),
        P(),
        P(),
    )
    return jax.shard_map(
        shards,
        mesh=mesh,
        in_specs=placed,
        out_specs=(
            P(None, ("grp", "gx"), ("gy", "row"), None),
            P(None, ("grp", "gx"), ("gy", "row"), None),
        ),
        check_vma=False,
    )
```

profile of v0, /device:TPU:0, one launch (start us, length us, event | category | flops | bytes accessed | tf_op | source)
XLA Modules:
  0.0 119.9 jit_solution(14529348477892977606)
XLA Ops:
  0.7 2.9 %fusion.45 = f32[512,1024]{1,0:T(8,128)S(1)} fusion(s32[1024,64]{0,1:T(8,128)} %param.12, f32[8,8,4,128]{3,2,1,0:T(4,128)} %bitcast.141), kind=kOutput, calls=%fused_computation.45 | convolution fusion | flops 402784256 | bytes 2490368 | tf_op jit(solution)/shard_map/dot_general | solution.py:69
  3.6 2.4 %fusion.11 = f32[64,512]{1,0:T(8,128)S(1)} fusion(f32[512,1024]{1,0:T(8,128)S(1)} %fusion.45, f32[1024]{0:T(1024)S(1)} %copy-done.5, s32[64,1024]{1,0:T(8,128)S(1)} %copy-done.2, f32[8,8,4,128]{3,2,1,0:T(4,128)S(1)} %bitcast.142), kind=kOutput, calls=%fused_computation.13 | convolution fusion | flops 403308544 | bytes 2625536 | tf_op jit(solution)/shard_map/dot_general | solution.py:88
  6.1 1.3 %collective-permute-start = (f32[64,1,1,128]{3,2,0,1:T(1,128)S(1)}, f32[64,1,1,128]{3,2,0,1:T(1,128)S(1)}, u32[]{:S(2)}, u32[]{:S(2)}) collective-permute-start(f32[64,1,1,128]{3,2,0,1:T(1,128)S(1)} %get-tuple-element.49), channel_id=1, source_target_pairs={{1,0},{2,1},{3,2},{5,4},{6,5},{7,6},{9,8},{10,9},{11,10},{13,12},{... | collective-permute-start | bytes 98312 | tf_op jit(solution)/shard_map/ppermute | solution.py:22
  7.4 3.0 %collective-permute-start.1 = (f32[64,1,1,128]{3,2,0,1:T(1,128)S(1)}, f32[64,1,1,128]{3,2,0,1:T(1,128)S(1)}, u32[]{:S(2)}, u32[]{:S(2)}) collective-permute-start(f32[64,1,1,128]{3,2,0,1:T(1,128)S(1)} %get-tuple-element.48), channel_id=1, source_target_pairs={{0,1},{1,2},{2,3},{4,5},{5,6},{6,7},{8,9},{9,10},{10,11},{12,13},{... | collective-permute-start | bytes 98312 | tf_op jit(solution)/shard_map/ppermute | solution.py:19
  10.4 6.4 %all-to-all-start.4 = ((f32[1,64,1,4,128]{4,3,2,0,1:T(4,128)}), f32[1,64,1,4,128]{4,3,2,0,1:T(4,128)S(1)}, u32[]{:S(2)}, u32[]{:S(2)}) async-start(f32[1,64,1,4,128]{4,3,2,0,1:T(4,128)} %bitcast.26), calls=%async_computation.4 | async-start | bytes 262144 | tf_op jit(solution)/shard_map/all_to_all | solution.py:38
  16.9 0.5 select_maximum_fusion.6
  17.4 0.9 fusion.69
  18.3 5.2 %all-to-all-done.4 = f32[1,64,1,4,128]{4,3,2,0,1:T(4,128)S(1)} async-done(((f32[1,64,1,4,128]{4,3,2,0,1:T(4,128)}), f32[1,64,1,4,128]{4,3,2,0,1:T(4,128)S(1)}, u32[]{:S(2)}, u32[]{:S(2)}) %all-to-all-start.4) | async-done | bytes 131104 | tf_op jit(solution)/shard_map/all_to_all | solution.py:38
  23.4 3.4 %all-to-all-start = ((f32[1,64,1,4,128]{4,3,2,0,1:T(4,128)}), f32[1,64,1,4,128]{4,3,2,0,1:T(4,128)S(1)}, u32[]{:S(2)}, u32[]{:S(2)}) async-start(f32[1,64,1,4,128]{4,3,2,0,1:T(4,128)} %fusion.69), calls=%async_computation | async-start | bytes 262144 | tf_op jit(solution)/shard_map/all_to_all | solution.py:38
  26.9 0.6 broadcast_compare_fusion
  27.5 5.6 %all-to-all-done = f32[1,64,1,4,128]{4,3,2,0,1:T(4,128)S(1)} async-done(((f32[1,64,1,4,128]{4,3,2,0,1:T(4,128)}), f32[1,64,1,4,128]{4,3,2,0,1:T(4,128)S(1)}, u32[]{:S(2)}, u32[]{:S(2)}) %all-to-all-start) | async-done | bytes 131104 | tf_op jit(solution)/shard_map/all_to_all | solution.py:38
  33.4 0.6 fusion.112
  34.0 0.4 pad.120
  34.5 0.4 pad.125
  34.9 0.4 pad.124
  35.3 0.4 pad.121
  35.8 1.3 %select_bitcast_fusion.3 = f32[1,16,4,4,128]{4,3,1,0,2:T(4,128)} fusion(f32[16,4,4,128]{3,2,0,1:T(4,128)S(1)} %add.277, f32[16,4,4,128]{3,2,0,1:T(4,128)S(1)} %pad.120, f32[16,4,4,128]{3,2,0,1:T(4,128)S(1)} %pad.121, pred[4,128]{1,0:T(4,128)(4,1)} %get-tuple-element.76), kind=kLoop, calls=%fused_computation.96 | loop fusion | flops 65536 | bytes 524800 | tf_op jit(solution)/shard_map/stack | solution.py:41
  37.1 3.3 %all-to-all-start.1 = ((f32[1,16,4,4,128]{4,3,1,0,2:T(4,128)}), f32[1,16,4,4,128]{4,3,1,0,2:T(4,128)S(1)}, u32[]{:S(2)}, u32[]{:S(2)}) async-start(f32[1,16,4,4,128]{4,3,1,0,2:T(4,128)} %select_bitcast_fusion.3), calls=%async_computation.1 | async-start | bytes 262144 | tf_op jit(solution)/shard_map/all_to_all | solution.py:42
  40.4 0.8 pad_maximum_fusion.12
  41.2 0.4 pad.137
  41.6 0.4 pad.142
  42.0 0.8 pad_maximum_fusion.13
  42.8 0.4 pad.141
  43.3 0.4 pad.138
  43.7 1.4 %select_bitcast_fusion.1 = f32[1,16,4,4,128]{4,3,1,0,2:T(4,128)} fusion(f32[16,4,4,128]{3,2,0,1:T(4,128)S(1)} %add.302, f32[16,4,4,128]{3,2,0,1:T(4,128)S(1)} %pad.137, f32[16,4,4,128]{3,2,0,1:T(4,128)S(1)} %pad.138, pred[4,128]{1,0:T(4,128)(4,1)} %get-tuple-element.75), kind=kLoop, calls=%fused_computation.92 | loop fusion | flops 65536 | bytes 524800 | tf_op jit(solution)/shard_map/stack | solution.py:41
  45.1 1.2 %all-to-all-done.1 = f32[1,16,4,4,128]{4,3,1,0,2:T(4,128)S(1)} async-done(((f32[1,16,4,4,128]{4,3,1,0,2:T(4,128)}), f32[1,16,4,4,128]{4,3,1,0,2:T(4,128)S(1)}, u32[]{:S(2)}, u32[]{:S(2)}) %all-to-all-start.1) | async-done | bytes 131104 | tf_op jit(solution)/shard_map/all_to_all | solution.py:42
  46.3 3.8 %all-to-all-start.5 = ((f32[1,16,4,4,128]{4,3,1,0,2:T(4,128)}), f32[1,16,4,4,128]{4,3,1,0,2:T(4,128)S(1)}, u32[]{:S(2)}, u32[]{:S(2)}) async-start(f32[1,16,4,4,128]{4,3,1,0,2:T(4,128)} %select_bitcast_fusion.1), calls=%async_computation.5 | async-start | bytes 262144 | tf_op jit(solution)/shard_map/all_to_all | solution.py:42
  50.1 1.8 %fusion.43 = f32[512,1024]{1,0:T(8,128)S(1)} fusion(s32[1024,64]{0,1:T(8,128)S(1)} %copy-done.3, f32[8,8,4,128]{3,2,1,0:T(4,128)S(1)} %bitcast.135), kind=kOutput, calls=%fused_computation.43 | convolution fusion | flops 402784256 | bytes 2490368 | tf_op jit(solution)/shard_map/dot_general | solution.py:69
  52.0 1.3 %copy-done = f32[512,1024]{1,0:T(8,128)} copy-done((f32[512,1024]{1,0:T(8,128)}, f32[512,1024]{1,0:T(8,128)S(1)}, u32[]{:S(2)}) %copy-start) | copy-done | bytes 2097176
  53.4 2.4 %fusion.8 = f32[64,512]{1,0:T(8,128)S(1)} fusion(f32[512,1024]{1,0:T(8,128)S(1)} %fusion.43, f32[1024]{0:T(1024)S(1)} %copy-done.5, s32[64,1024]{1,0:T(8,128)S(1)} %copy-done.2, f32[8,8,4,128]{3,2,1,0:T(4,128)S(1)} %bitcast.136), kind=kOutput, calls=%fused_computation.10 | convolution fusion | flops 403308544 | bytes 2625536 | tf_op jit(solution)/shard_map/dot_general | solution.py:88
  55.8 1.3 %collective-permute-start.2 = (f32[64,1,1,128]{3,2,0,1:T(1,128)S(1)}, f32[64,1,1,128]{3,2,0,1:T(1,128)S(1)}, u32[]{:S(2)}, u32[]{:S(2)}) collective-permute-start(f32[64,1,1,128]{3,2,0,1:T(1,128)S(1)} %get-tuple-element.40), channel_id=1, source_target_pairs={{1,0},{2,1},{3,2},{5,4},{6,5},{7,6},{9,8},{10,9},{11,10},{13,12},{... | collective-permute-start | bytes 98312 | tf_op jit(solution)/shard_map/ppermute | solution.py:22
  57.1 3.0 %collective-permute-start.3 = (f32[64,1,1,128]{3,2,0,1:T(1,128)S(1)}, f32[64,1,1,128]{3,2,0,1:T(1,128)S(1)}, u32[]{:S(2)}, u32[]{:S(2)}) collective-permute-start(f32[64,1,1,128]{3,2,0,1:T(1,128)S(1)} %get-tuple-element.39), channel_id=1, source_target_pairs={{0,1},{1,2},{2,3},{4,5},{5,6},{6,7},{8,9},{9,10},{10,11},{12,13},{... | collective-permute-start | bytes 98312 | tf_op jit(solution)/shard_map/ppermute | solution.py:19
  60.2 0.8 collective-permute-done.3
  61.0 1.3 %select_maximum_fusion.4 = f32[64,1,6,130]{3,2,0,1:T(8,128)} fusion(f32[64,1,1,128]{3,2,0,1:T(1,128)S(1)} %collective-permute-done.2, f32[64,1,4,128]{3,2,0,1:T(4,128)S(1)} %reshape.117, f32[64,1,1,128]{3,2,0,1:T(1,128)S(1)} %collective-permute-done.3), kind=kLoop, calls=%fused_computation.30 | loop fusion | flops 399360 | bytes 396288 | tf_op jit(solution)/shard_map/concatenate | solution.py:23
  62.3 2.0 %broadcast_multiply_fusion.1 = (f32[64,1,4,128]{3,2,0,1:T(4,128)S(1)}, f32[1,64,1,4,128]{4,3,2,0,1:T(4,128)}) fusion(f32[64,1,4,128]{3,2,0,1:T(4,128)S(1)} %bitcast.159, f32[4,128]{1,0:T(4,128)S(1)} %copy-done.9, f32[64,1,4,128]{3,2,0,1:T(4,128)S(1)} %reshape.117, f32[64,1,6,130]{3,2,0,1:T(8,128)} %select_maximum_fusion.4, ...), kind=kLoop, calls=%fused_computation.146 | loop fusion | flops 360448 | bytes 854016 | tf_op jit(solution)/shard_map/mul | solution.py:106
  64.4 1.3 %collective-permute-start.4 = (f32[64,1,1,128]{3,2,0,1:T(1,128)S(1)}, f32[64,1,1,128]{3,2,0,1:T(1,128)S(1)}, u32[]{:S(2)}, u32[]{:S(2)}) collective-permute-start(f32[64,1,1,128]{3,2,0,1:T(1,128)S(1)} %get-tuple-element.24), channel_id=1, source_target_pairs={{1,0},{2,1},{3,2},{5,4},{6,5},{7,6},{9,8},{10,9},{11,10},{13,12},{... | collective-permute-start | bytes 98312 | tf_op jit(solution)/shard_map/ppermute | solution.py:22
  65.7 3.0 %collective-permute-start.5 = (f32[64,1,1,128]{3,2,0,1:T(1,128)S(1)}, f32[64,1,1,128]{3,2,0,1:T(1,128)S(1)}, u32[]{:S(2)}, u32[]{:S(2)}) collective-permute-start(f32[64,1,1,128]{3,2,0,1:T(1,128)S(1)} %get-tuple-element.23), channel_id=1, source_target_pairs={{0,1},{1,2},{2,3},{4,5},{5,6},{6,7},{8,9},{9,10},{10,11},{12,13},{... | collective-permute-start | bytes 98312 | tf_op jit(solution)/shard_map/ppermute | solution.py:19
  68.7 5.1 %all-to-all-start.2 = ((f32[1,64,1,4,128]{4,3,2,0,1:T(4,128)}), f32[1,64,1,4,128]{4,3,2,0,1:T(4,128)S(1)}, u32[]{:S(2)}, u32[]{:S(2)}) async-start(f32[1,64,1,4,128]{4,3,2,0,1:T(4,128)} %get-tuple-element.74), calls=%async_computation.2 | async-start | bytes 262144 | tf_op jit(solution)/shard_map/all_to_all | solution.py:38
  73.8 0.5 select_maximum_fusion.2
  74.5 1.8 %fusion.37 = f32[512,1024]{1,0:T(8,128)S(1)} fusion(s32[64,1024]{1,0:T(8,128)S(1)} %copy-done.2, f32[8,8,4,128]{3,2,1,0:T(4,128)S(1)} %bitcast.148), kind=kOutput, calls=%fused_computation.37 | convolution fusion | flops 402718720 | bytes 2490368 | tf_op jit(solution)/shard_map/dot_general | solution.py:94
  76.4 2.5 %fusion.18 = f32[64,512]{1,0:T(8,128)S(1)} fusion(f32[512,1024]{1,0:T(8,128)S(1)} %fusion.37, f32[512,1024]{1,0:T(8,128)S(1)} %copy-done.1, f32[1024]{0:T(1024)S(1)} %copy-done.5, s32[1024,64]{0,1:T(8,128)S(1)} %copy-done.3, f32[8,8,4,128]{3,2,1,0:T(4,128)S(1)} %bitcast.149, f32[8,8,4,128]{3,2,1,0:T(4,128)S(1)} %bitcast.137), kind=kOutput, calls=%fused_computation.16 | convolution fusion | flops 403963904 | bytes 4853760 | tf_op jit(solution)/shard_map/dot_general | solution.py:95
  78.9 0.9 all-to-all-done.2
  79.8 10.6 %all_to_all.120 = f32[1,64,1,4,128]{4,3,2,0,1:T(4,128)S(1)} all-to-all(f32[1,64,1,4,128]{4,3,2,0,1:T(4,128)S(1)} %bitcast.158), channel_id=1, replica_groups=mesh['grp'=2,'gx'=4,'gy'=2,'row'=2] {'gx'}, dimensions={1} | all-to-all | bytes 262144 | tf_op jit(solution)/shard_map/all_to_all | solution.py:38
  90.6 0.7 fusion.110
  91.3 0.4 pad.147
  91.8 0.4 pad.146
  92.6 0.4 pad.150
  93.1 1.4 %select_bitcast_fusion = f32[1,16,4,4,128]{4,3,1,0,2:T(4,128)} fusion(f32[16,4,4,128]{3,2,0,1:T(4,128)S(1)} %add.318, f32[16,4,4,128]{3,2,0,1:T(4,128)S(1)} %pad.146, f32[16,4,4,128]{3,2,0,1:T(4,128)S(1)} %pad.147, pred[4,128]{1,0:T(4,128)(4,1)} %get-tuple-element.75), kind=kLoop, calls=%fused_computation.91 | loop fusion | flops 65536 | bytes 524800 | tf_op jit(solution)/shard_map/stack | solution.py:41
  94.5 3.4 %all-to-all-start.7 = ((f32[1,16,4,4,128]{4,3,1,0,2:T(4,128)}), f32[1,16,4,4,128]{4,3,1,0,2:T(4,128)S(1)}, u32[]{:S(2)}, u32[]{:S(2)}) async-start(f32[1,16,4,4,128]{4,3,1,0,2:T(4,128)} %select_bitcast_fusion), calls=%async_computation.7 | async-start | bytes 262144 | tf_op jit(solution)/shard_map/all_to_all | solution.py:42
  98.2 0.8 pad_maximum_fusion.10
  99.0 0.4 pad.129
  99.5 0.4 pad.134
  99.9 0.4 pad.133
  100.4 0.7 select_bitcast_fusion.2
  101.1 3.2 %all-to-all-done.7 = f32[1,16,4,4,128]{4,3,1,0,2:T(4,128)S(1)} async-done(((f32[1,16,4,4,128]{4,3,1,0,2:T(4,128)}), f32[1,16,4,4,128]{4,3,1,0,2:T(4,128)S(1)}, u32[]{:S(2)}, u32[]{:S(2)}) %all-to-all-start.7) | async-done | bytes 131104 | tf_op jit(solution)/shard_map/all_to_all | solution.py:42
  104.2 3.3 %all-to-all-start.3 = ((f32[1,16,4,4,128]{4,3,1,0,2:T(4,128)}), f32[1,16,4,4,128]{4,3,1,0,2:T(4,128)S(1)}, u32[]{:S(2)}, u32[]{:S(2)}) async-start(f32[1,16,4,4,128]{4,3,1,0,2:T(4,128)} %select_bitcast_fusion.2), calls=%async_computation.3 | async-start | bytes 262144 | tf_op jit(solution)/shard_map/all_to_all | solution.py:42
  107.7 1.3 %collective-permute-start.6 = (f32[64,1,1,128]{3,2,0,1:T(1,128)S(1)}, f32[64,1,1,128]{3,2,0,1:T(1,128)S(1)}, u32[]{:S(2)}, u32[]{:S(2)}) collective-permute-start(f32[64,1,1,128]{3,2,0,1:T(1,128)S(1)} %get-tuple-element.15), channel_id=1, source_target_pairs={{1,0},{2,1},{3,2},{5,4},{6,5},{7,6},{9,8},{10,9},{11,10},{13,12},{... | collective-permute-start | bytes 98312 | tf_op jit(solution)/shard_map/ppermute | solution.py:22
  109.0 3.0 %collective-permute-start.7 = (f32[64,1,1,128]{3,2,0,1:T(1,128)S(1)}, f32[64,1,1,128]{3,2,0,1:T(1,128)S(1)}, u32[]{:S(2)}, u32[]{:S(2)}) collective-permute-start(f32[64,1,1,128]{3,2,0,1:T(1,128)S(1)} %get-tuple-element.14), channel_id=1, source_target_pairs={{0,1},{1,2},{2,3},{4,5},{5,6},{6,7},{8,9},{9,10},{10,11},{12,13},{... | collective-permute-start | bytes 98312 | tf_op jit(solution)/shard_map/ppermute | solution.py:19
  112.0 1.4 %all-to-all-done.3 = f32[1,16,4,4,128]{4,3,1,0,2:T(4,128)S(1)} async-done(((f32[1,16,4,4,128]{4,3,1,0,2:T(4,128)}), f32[1,16,4,4,128]{4,3,1,0,2:T(4,128)S(1)}, u32[]{:S(2)}, u32[]{:S(2)}) %all-to-all-start.3) | async-done | bytes 131104 | tf_op jit(solution)/shard_map/all_to_all | solution.py:42
  113.5 0.5 select_maximum_fusion
  114.2 1.8 %fusion.35 = f32[512,1024]{1,0:T(8,128)S(1)} fusion(s32[64,1024]{1,0:T(8,128)S(1)} %copy-done.2, f32[8,8,4,128]{3,2,1,0:T(4,128)S(1)} %bitcast.150), kind=kOutput, calls=%fused_computation.35 | convolution fusion | flops 402718720 | bytes 2490368 | tf_op jit(solution)/shard_map/dot_general | solution.py:94
  116.0 2.5 %fusion.27 = f32[64,512]{1,0:T(8,128)S(1)} fusion(f32[512,1024]{1,0:T(8,128)S(1)} %fusion.35, f32[512,1024]{1,0:T(8,128)S(1)} %fusion.45, f32[1024]{0:T(1024)S(1)} %copy-done.5, s32[1024,64]{0,1:T(8,128)S(1)} %copy-done.3, f32[8,8,4,128]{3,2,1,0:T(4,128)S(1)} %bitcast.151, f32[8,8,4,128]{3,2,1,0:T(4,128)S(1)} %bitcast.143), kind=kOutput, calls=%fused_computation.19 | convolution fusion | flops 403963904 | bytes 4853760 | tf_op jit(solution)/shard_map/dot_general | solution.py:95
  118.5 0.7 reshape.120
  119.2 0.7 copy.44
  (83 shorter events, 2.4 us)
Async XLA Ops:
  0.6 3.0 %copy-start.4 = (f32[64,1,4,128]{3,2,1,0:T(4,128)S(1)}, f32[64,1,4,128]{3,2,1,0:T(4,128)}, u32[]{:S(2)}) copy-start(f32[64,1,4,128]{3,2,1,0:T(4,128)} %param.7) | copy-start | bytes 393220
  0.6 3.0 %copy-start.5 = (f32[1024]{0:T(1024)S(1)}, f32[1024]{0:T(1024)}, u32[]{:S(2)}) copy-start(f32[1024]{0:T(1024)} %param.11) | copy-start | bytes 12292
  0.6 3.0 %copy-start.2 = (s32[64,1024]{1,0:T(8,128)S(1)}, s32[64,1024]{1,0:T(8,128)}, u32[]{:S(2)}) copy-start(s32[64,1024]{1,0:T(8,128)} %param.13) | copy-start | bytes 786436
  3.6 13.2 %copy-start.13 = (f32[4,128]{1,0:T(4,128)S(1)}, f32[4,128]{1,0:T(4,128)}, u32[]{:S(2)}) copy-start(f32[4,128]{1,0:T(4,128)} %param.9) | copy-start | bytes 6148
  3.6 23.3 %copy-start.12 = (s32[4,128]{1,0:T(4,128)S(1)}, s32[4,128]{1,0:T(4,128)}, u32[]{:S(2)}) copy-start(s32[4,128]{1,0:T(4,128)} %param.10) | copy-start | bytes 6148
  6.1 10.8 %collective-permute-start = (f32[64,1,1,128]{3,2,0,1:T(1,128)S(1)}, f32[64,1,1,128]{3,2,0,1:T(1,128)S(1)}, u32[]{:S(2)}, u32[]{:S(2)}) collective-permute-start(f32[64,1,1,128]{3,2,0,1:T(1,128)S(1)} %get-tuple-element.49), channel_id=1, source_target_pairs={{1,0},{2,1},{3,2},{5,4},{6,5},{7,6},{9,8},{10,9},{11,10},{13,12},{... | collective-permute-start | bytes 98312 | tf_op jit(solution)/shard_map/ppermute | solution.py:22
  7.4 9.5 %collective-permute-start.1 = (f32[64,1,1,128]{3,2,0,1:T(1,128)S(1)}, f32[64,1,1,128]{3,2,0,1:T(1,128)S(1)}, u32[]{:S(2)}, u32[]{:S(2)}) collective-permute-start(f32[64,1,1,128]{3,2,0,1:T(1,128)S(1)} %get-tuple-element.48), channel_id=1, source_target_pairs={{0,1},{1,2},{2,3},{4,5},{5,6},{6,7},{8,9},{9,10},{10,11},{12,13},{... | collective-permute-start | bytes 98312 | tf_op jit(solution)/shard_map/ppermute | solution.py:19
  10.4 13.0 %all-to-all-start.4 = ((f32[1,64,1,4,128]{4,3,2,0,1:T(4,128)}), f32[1,64,1,4,128]{4,3,2,0,1:T(4,128)S(1)}, u32[]{:S(2)}, u32[]{:S(2)}) async-start(f32[1,64,1,4,128]{4,3,2,0,1:T(4,128)} %bitcast.26), calls=%async_computation.4 | async-start | bytes 262144 | tf_op jit(solution)/shard_map/all_to_all | solution.py:38
  16.8 16.4 %copy-start.8 = (f32[4,128]{1,0:T(4,128)}, f32[4,128]{1,0:T(4,128)S(1)}, u32[]{:S(2)}) copy-start(f32[4,128]{1,0:T(4,128)S(1)} %get-tuple-element.82) | copy-start | bytes 6148
  16.9 16.4 %copy-start.6 = (f32[2,4,128]{2,1,0:T(4,128)}, f32[2,4,128]{2,1,0:T(4,128)S(1)}, u32[]{:S(2)}) copy-start(f32[2,4,128]{2,1,0:T(4,128)S(1)} %reverse_bitcast_fusion) | copy-start | bytes 12292
  23.4 9.6 %all-to-all-start = ((f32[1,64,1,4,128]{4,3,2,0,1:T(4,128)}), f32[1,64,1,4,128]{4,3,2,0,1:T(4,128)S(1)}, u32[]{:S(2)}, u32[]{:S(2)}) async-start(f32[1,64,1,4,128]{4,3,2,0,1:T(4,128)} %fusion.69), calls=%async_computation | async-start | bytes 262144 | tf_op jit(solution)/shard_map/all_to_all | solution.py:38
  34.5 15.7 %copy-start.3 = (s32[1024,64]{0,1:T(8,128)S(1)}, s32[1024,64]{0,1:T(8,128)}, u32[]{:S(2)}) copy-start(s32[1024,64]{0,1:T(8,128)} %param.12) | copy-start | bytes 786436
  37.1 9.2 %all-to-all-start.1 = ((f32[1,16,4,4,128]{4,3,1,0,2:T(4,128)}), f32[1,16,4,4,128]{4,3,1,0,2:T(4,128)S(1)}, u32[]{:S(2)}, u32[]{:S(2)}) async-start(f32[1,16,4,4,128]{4,3,1,0,2:T(4,128)} %select_bitcast_fusion.3), calls=%async_computation.1 | async-start | bytes 262144 | tf_op jit(solution)/shard_map/all_to_all | solution.py:42
  46.3 16.0 %all-to-all-start.5 = ((f32[1,16,4,4,128]{4,3,1,0,2:T(4,128)}), f32[1,16,4,4,128]{4,3,1,0,2:T(4,128)S(1)}, u32[]{:S(2)}, u32[]{:S(2)}) async-start(f32[1,16,4,4,128]{4,3,1,0,2:T(4,128)} %select_bitcast_fusion.1), calls=%async_computation.5 | async-start | bytes 262144 | tf_op jit(solution)/shard_map/all_to_all | solution.py:42
  52.0 1.3 %copy-start = (f32[512,1024]{1,0:T(8,128)}, f32[512,1024]{1,0:T(8,128)S(1)}, u32[]{:S(2)}) copy-start(f32[512,1024]{1,0:T(8,128)S(1)} %fusion.43) | copy-start | bytes 6291460
  53.4 8.9 %copy-start.9 = (f32[4,128]{1,0:T(4,128)S(1)}, f32[4,128]{1,0:T(4,128)}, u32[]{:S(2)}) copy-start(f32[4,128]{1,0:T(4,128)} %copy-done.8) | copy-start | bytes 6148
  55.8 4.3 %collective-permute-start.2 = (f32[64,1,1,128]{3,2,0,1:T(1,128)S(1)}, f32[64,1,1,128]{3,2,0,1:T(1,128)S(1)}, u32[]{:S(2)}, u32[]{:S(2)}) collective-permute-start(f32[64,1,1,128]{3,2,0,1:T(1,128)S(1)} %get-tuple-element.40), channel_id=1, source_target_pairs={{1,0},{2,1},{3,2},{5,4},{6,5},{7,6},{9,8},{10,9},{11,10},{13,12},{... | collective-permute-start | bytes 98312 | tf_op jit(solution)/shard_map/ppermute | solution.py:22
  57.1 3.9 %collective-permute-start.3 = (f32[64,1,1,128]{3,2,0,1:T(1,128)S(1)}, f32[64,1,1,128]{3,2,0,1:T(1,128)S(1)}, u32[]{:S(2)}, u32[]{:S(2)}) collective-permute-start(f32[64,1,1,128]{3,2,0,1:T(1,128)S(1)} %get-tuple-element.39), channel_id=1, source_target_pairs={{0,1},{1,2},{2,3},{4,5},{5,6},{6,7},{8,9},{9,10},{10,11},{12,13},{... | collective-permute-start | bytes 98312 | tf_op jit(solution)/shard_map/ppermute | solution.py:19
  64.4 9.4 %collective-permute-start.4 = (f32[64,1,1,128]{3,2,0,1:T(1,128)S(1)}, f32[64,1,1,128]{3,2,0,1:T(1,128)S(1)}, u32[]{:S(2)}, u32[]{:S(2)}) collective-permute-start(f32[64,1,1,128]{3,2,0,1:T(1,128)S(1)} %get-tuple-element.24), channel_id=1, source_target_pairs={{1,0},{2,1},{3,2},{5,4},{6,5},{7,6},{9,8},{10,9},{11,10},{13,12},{... | collective-permute-start | bytes 98312 | tf_op jit(solution)/shard_map/ppermute | solution.py:22
  65.7 8.1 %collective-permute-start.5 = (f32[64,1,1,128]{3,2,0,1:T(1,128)S(1)}, f32[64,1,1,128]{3,2,0,1:T(1,128)S(1)}, u32[]{:S(2)}, u32[]{:S(2)}) collective-permute-start(f32[64,1,1,128]{3,2,0,1:T(1,128)S(1)} %get-tuple-element.23), channel_id=1, source_target_pairs={{0,1},{1,2},{2,3},{4,5},{5,6},{6,7},{8,9},{9,10},{10,11},{12,13},{... | collective-permute-start | bytes 98312 | tf_op jit(solution)/shard_map/ppermute | solution.py:19
  68.7 11.1 %all-to-all-start.2 = ((f32[1,64,1,4,128]{4,3,2,0,1:T(4,128)}), f32[1,64,1,4,128]{4,3,2,0,1:T(4,128)S(1)}, u32[]{:S(2)}, u32[]{:S(2)}) async-start(f32[1,64,1,4,128]{4,3,2,0,1:T(4,128)} %get-tuple-element.74), calls=%async_computation.2 | async-start | bytes 262144 | tf_op jit(solution)/shard_map/all_to_all | solution.py:38
  73.8 2.6 %copy-start.1 = (f32[512,1024]{1,0:T(8,128)S(1)}, f32[512,1024]{1,0:T(8,128)}, u32[]{:S(2)}) copy-start(f32[512,1024]{1,0:T(8,128)} %copy-done) | copy-start | bytes 6291460
  76.4 14.1 %copy-start.7 = (f32[2,4,128]{2,1,0:T(4,128)S(1)}, f32[2,4,128]{2,1,0:T(4,128)}, u32[]{:S(2)}) copy-start(f32[2,4,128]{2,1,0:T(4,128)} %copy-done.6) | copy-start | bytes 12292
  91.3 9.0 %copy-start.11 = (pred[4,128]{1,0:T(4,128)(4,1)S(1)}, pred[4,128]{1,0:T(4,128)(4,1)}, u32[]{:S(2)}) copy-start(pred[4,128]{1,0:T(4,128)(4,1)} %get-tuple-element.76) | copy-start | bytes 1540
  91.8 15.8 %copy-start.10 = (f32[4,128]{1,0:T(4,128)S(1)}, f32[4,128]{1,0:T(4,128)}, u32[]{:S(2)}) copy-start(f32[4,128]{1,0:T(4,128)} %copy-done.8) | copy-start | bytes 6148
  94.5 9.8 %all-to-all-start.7 = ((f32[1,16,4,4,128]{4,3,1,0,2:T(4,128)}), f32[1,16,4,4,128]{4,3,1,0,2:T(4,128)S(1)}, u32[]{:S(2)}, u32[]{:S(2)}) async-start(f32[1,16,4,4,128]{4,3,1,0,2:T(4,128)} %select_bitcast_fusion), calls=%async_computation.7 | async-start | bytes 262144 | tf_op jit(solution)/shard_map/all_to_all | solution.py:42
  104.2 9.2 %all-to-all-start.3 = ((f32[1,16,4,4,128]{4,3,1,0,2:T(4,128)}), f32[1,16,4,4,128]{4,3,1,0,2:T(4,128)S(1)}, u32[]{:S(2)}, u32[]{:S(2)}) async-start(f32[1,16,4,4,128]{4,3,1,0,2:T(4,128)} %select_bitcast_fusion.2), calls=%async_computation.3 | async-start | bytes 262144 | tf_op jit(solution)/shard_map/all_to_all | solution.py:42
  107.7 5.8 %collective-permute-start.6 = (f32[64,1,1,128]{3,2,0,1:T(1,128)S(1)}, f32[64,1,1,128]{3,2,0,1:T(1,128)S(1)}, u32[]{:S(2)}, u32[]{:S(2)}) collective-permute-start(f32[64,1,1,128]{3,2,0,1:T(1,128)S(1)} %get-tuple-element.15), channel_id=1, source_target_pairs={{1,0},{2,1},{3,2},{5,4},{6,5},{7,6},{9,8},{10,9},{11,10},{13,12},{... | collective-permute-start | bytes 98312 | tf_op jit(solution)/shard_map/ppermute | solution.py:22
  109.0 4.5 %collective-permute-start.7 = (f32[64,1,1,128]{3,2,0,1:T(1,128)S(1)}, f32[64,1,1,128]{3,2,0,1:T(1,128)S(1)}, u32[]{:S(2)}, u32[]{:S(2)}) collective-permute-start(f32[64,1,1,128]{3,2,0,1:T(1,128)S(1)} %get-tuple-element.14), channel_id=1, source_target_pairs={{0,1},{1,2},{2,3},{4,5},{5,6},{6,7},{8,9},{9,10},{10,11},{12,13},{... | collective-permute-start | bytes 98312 | tf_op jit(solution)/shard_map/ppermute | solution.py:19
where the time goes:
time: 121 us; the launch traced here: 120 us
  starting transfers between devices  46 us (38%)
  waiting for transfers between devices  18.3 us (15%)
  matrix products  18.1 us (15%)
  other arithmetic  15.8 us (13%)
  blocking collectives  10.6 us (9%)
  local copies, waits for them, and re-layouts  9.78 us (8%)
  between operations  1.26 us (1%)
    all_to_all x3, starting transfers between devices, sweep_fields(): lax.all_to_all(stacked, 'gx', split_axis=1, concat_axis=2, tiled=True)  14.9 us
    all_to_all x4, starting transfers between devices, sweep_fields(): lax.all_to_all(results, 'gx', split_axis=2, concat_axis=1, tiled=True)  13.9 us
    ppermute x4, starting transfers between devices, padded_2(): lax.ppermute(lax.slice_in_dim(block, block.shape[dim] - width, None, axis...  12.1 us
    all_to_all x3, waiting for transfers between devices, sweep_fields(): lax.all_to_all(stacked, 'gx', split_axis=1, concat_axis=2, tiled=True)  11.7 us
    all_to_all x1, blocking collectives, sweep_fields(): lax.all_to_all(stacked, 'gx', split_axis=1, concat_axis=2, tiled=True)  10.6 us
    pad x16, local copies, waits for them, and re-layouts, recurrence(): lax.associative_scan(combine_pairs, (multipliers, values), reverse=backwa...  6.67 us
    all_to_all x4, waiting for transfers between devices, sweep_fields(): lax.all_to_all(results, 'gx', split_axis=2, concat_axis=1, tiled=True)  5.84 us
    ppermute x4, starting transfers between devices, padded_2(): lax.ppermute(lax.slice_in_dim(block, 0, width, axis=dim), axis, backward)  5.17 us
  transfers between devices with their start and end apart: 15, of which 7 were waited for; matrix products, arithmetic and copies ran while one was open for 17% of the time, Pallas kernels for 0%

commit v1 on v0

v1 whole, which is shorter than its diff:
```python
import functools

import jax
import jax.numpy as jnp
from jax import lax
from jax.experimental import pallas as pl
from jax.experimental.pallas import tpu as pltpu
from jax.sharding import PartitionSpec as P

MESH = pl.DeviceIdType.MESH
F32 = jnp.float32
BF16 = jnp.bfloat16
TIME_STEP = 0.1
DIFFUSION = 0.1
HALF_LOG2E = 0.5 * 1.4426950408889634
FWD0, ADJ1, FWD1, ADJ0 = range(4)


def kernel(
    sizes, conc_hbm, cot_hbm, cour_ref, dir_ref, const_ref, ord_hbm, sto_hbm, fin_hbm, adj_hbm,
    conc, cot, state, spread, field, values, recv, sent, halo, out_fin, out_adj, rates0, rates_b, grad_b,
    ord_i, sto_i, ord2, ord_t, sto2, sto, log_k,
    in_sem, tab_sem, out_sem, send_sem, recv_sem, hsend_sem, hrecv_sem,
):
    nx, ngy, nrow = sizes
    ny = ngy * nrow
    depth, species, width = conc.shape
    reactions = ord_i.shape[1]
    edges = sorted({0, depth - 1})
    inner = list(range(1, depth - 1))
    groups = [g for g in (inner, edges) if g]
    order = [r for g in groups for r in g]
    chunk = min(256, reactions)

    x = lax.axis_index("gx")
    y = lax.axis_index("gy") * nrow + lax.axis_index("row")

    def line(target):
        return {"gy": lax.div(target, nrow), "row": lax.rem(target, nrow)}

    neighbours = [
        (x > 0, {"gx": x - 1}), (x < nx - 1, {"gx": x + 1}),
        (y > 0, line(y - 1)), (y < ny - 1, line(y + 1)),
    ]

    def load(item):
        source, target, base = item
        return [pltpu.make_async_copy(source.at[:, 0, r, :], target.at[r], in_sem.at[base, r]) for r in range(depth)]

    loads_cot = load((cot_hbm, cot, 0))
    loads_conc = load((conc_hbm, conc, 1))
    tables = [pltpu.make_async_copy(ord_hbm, ord_i, tab_sem.at[0]), pltpu.make_async_copy(sto_hbm, sto_i, tab_sem.at[1])]
    for copy in loads_cot + loads_conc + tables:
        copy.start()

    barrier = pltpu.get_barrier_semaphore()
    for there, device in neighbours:
        @pl.when(there)
        def _():
            pl.semaphore_signal(barrier, inc=1, device_id=device, device_id_type=MESH)

    @pl.when(x == 0)
    def _():
        for s in range(4):
            recv[s, 0] = jnp.zeros_like(recv[s, 0])

    @pl.when(x == nx - 1)
    def _():
        for s in range(4):
            recv[s, 1] = jnp.zeros_like(recv[s, 1])

    @pl.when(y == 0)
    def _():
        for s in range(4):
            halo[s, 0] = jnp.zeros_like(halo[s, 0])

    @pl.when(y == ny - 1)
    def _():
        for s in range(4):
            halo[s, 1] = jnp.zeros_like(halo[s, 1])

    courant = cour_ref[...]
    retain_all = courant / (1.0 + courant)
    admit_all = 1.0 / (1.0 + courant)
    retain = [retain_all[r:r + 1] for r in range(depth)]
    admit = [admit_all[r:r + 1] for r in range(depth)]
    rising = [jnp.broadcast_to(dir_ref[r:r + 1], (species, width)) for r in range(depth)]

    for copy in loads_cot:
        copy.wait()
    pl.semaphore_wait(barrier, sum(jnp.where(there, 1, 0) for there, _ in neighbours))

    one = jnp.where(x < (nx + 1) // 2, 0, 1)
    two = 1 - one

    def link(s, d, r):
        return pltpu.make_async_remote_copy(
            src_ref=sent.at[s, d, r], dst_ref=recv.at[s, d, r],
            send_sem=send_sem.at[s, d, r], recv_sem=recv_sem.at[s, d, r],
            device_id={"gx": x + 1 - 2 * d}, device_id_type=MESH,
        )

    def inside(position):
        return (position >= 0) & (position < nx)

    def relay(s, d, source, rows, arrive=True):
        pred, succ = inside(x - 1 + 2 * d), inside(x + 1 - 2 * d)
        for r in rows:
            if arrive:
                @pl.when(pred)
                def _():
                    link(s, d, r).wait_recv()
            sent[s, d, r] = source[r] + retain[r] * recv[s, d, r]

            @pl.when(succ)
            def _():
                link(s, d, r).start()

    first_end = jnp.logical_not(inside(x - 1 + 2 * one))

    def seed(s, source, rows):
        @pl.when(first_end)
        def _():
            relay(s, one, source, rows, arrive=False)

    def relay_first(s, source, rows):
        @pl.when(jnp.logical_not(first_end))
        def _():
            relay(s, one, source, rows)

    def chosen(s, r, adjoint):
        pick = (rising[r] == 0) if adjoint else (rising[r] == 1)
        return jnp.where(pick, sent[s, 0, r], sent[s, 1, r])

    def halo_copies(s):
        down = pltpu.make_async_remote_copy(
            src_ref=field.at[s, 0], dst_ref=halo.at[s, 1], send_sem=hsend_sem.at[s, 0], recv_sem=hrecv_sem.at[s, 1],
            device_id=line(y - 1), device_id_type=MESH)
        up = pltpu.make_async_remote_copy(
            src_ref=field.at[s, depth - 1], dst_ref=halo.at[s, 0], send_sem=hsend_sem.at[s, 1], recv_sem=hrecv_sem.at[s, 0],
            device_id=line(y + 1), device_id_type=MESH)
        return down, up

    def halo_send(s):
        @pl.when(y > 0)
        def _():
            halo_copies(s)[0].start()

        @pl.when(y < ny - 1)
        def _():
            halo_copies(s)[1].start()

    def halo_wait(s):
        @pl.when(y > 0)
        def _():
            halo_copies(s)[1].wait_recv()

        @pl.when(y < ny - 1)
        def _():
            halo_copies(s)[0].wait_recv()

    lane = lax.broadcasted_iota(jnp.int32, (species, width), 1)

    def smooth(s, r):
        here = field[s, r]
        below = halo[s, 0] if r == 0 else field[s, r - 1]
        above = halo[s, 1] if r == depth - 1 else field[s, r + 1]
        before = jnp.where(lane == 0, 0.0, pltpu.roll(here, 1, 1))
        after = jnp.where(lane == width - 1, 0.0, pltpu.roll(here, width - 1, 1))
        return here + DIFFUSION * (above + below + after + before - 4.0 * here)

    def side(parts):
        return parts[0] if len(parts) == 1 else jnp.concatenate(parts, axis=1)

    def split(value):
        high = value.astype(BF16)
        low = (value - high.astype(F32)).astype(BF16)
        return jnp.concatenate([high, low], axis=0)

    def activity(rows, source):
        return split(side([HALF_LOG2E * jnp.log(1.0 + source[r] * source[r]) for r in rows]))

    def rates_at(part, act, count):
        exponent = jnp.dot(ord2[part, :], act, preferred_element_type=F32)
        return jnp.exp2(exponent + side([log_k[part, :]] * count))

    parts = [pl.ds(i, chunk) for i in range(0, reactions, chunk)]

    def keep(target, part, cols, value):
        high = value.astype(BF16)
        target[0, part, cols] = high
        target[1, part, cols] = (value - high.astype(F32)).astype(BF16)

    def gather(table, halves, cols):
        small = jnp.dot(table[...], halves[1, :, cols], preferred_element_type=F32)
        return small + jnp.dot(table[...], halves[0, :, cols], preferred_element_type=F32)

    def columns(rows):
        start = order.index(rows[0]) * width
        return pl.ds(start, len(rows) * width)

    def put_react(rows, source, s, produced):
        for i, r in enumerate(rows):
            field[s, r] = source[r] + TIME_STEP * produced[:, i * width:(i + 1) * width]

    def react_first(rows):
        act, cols = activity(rows, conc), columns(rows)
        for part in parts:
            rates = rates_at(part, act, len(rows))
            rates0[part, cols] = rates
            keep(rates_b, part, cols, rates)
        put_react(rows, conc, FWD0, gather(sto, rates_b, cols))

    def put_back(rows, cells, summed, target):
        for i, r in enumerate(rows):
            c = cells[r]
            target[r] = spread[r] + TIME_STEP * c / (1.0 + c * c) * summed[:, i * width:(i + 1) * width]

    def react_both(rows):
        act, cols = activity(rows, state), columns(rows)
        push = split(side([spread[r] for r in rows]))
        for part in parts:
            rates = rates_at(part, act, len(rows))
            pulled = jnp.dot(sto2[part, :], push, preferred_element_type=F32)
            keep(rates_b, part, cols, rates)
            keep(grad_b, part, cols, rates * pulled)
        put_back(rows, state, gather(ord_t, grad_b, cols), values.at[1])
        seed(ADJ0, values.at[1], rows)
        put_react(rows, state, FWD1, gather(sto, rates_b, cols))

    def react_last(rows):
        cols = columns(rows)
        push = split(side([spread[r] for r in rows]))
        for part in parts:
            pulled = jnp.dot(sto2[part, :], push, preferred_element_type=F32)
            keep(grad_b, part, cols, rates0[part, cols] * pulled)
        put_back(rows, conc, gather(ord_t, grad_b, cols), out_adj)

    seed(ADJ1, cot, order)
    for copy in tables + loads_conc:
        copy.wait()
    order_float = ord_i[...].astype(F32)
    ord_t[...] = order_float.astype(BF16)
    order_trans = order_float.T.astype(BF16)
    ord2[:, :species] = order_trans
    ord2[:, species:] = order_trans
    stoich_float = sto_i[...].astype(F32)
    sto[...] = stoich_float.astype(BF16)
    stoich_trans = stoich_float.T.astype(BF16)
    sto2[:, :species] = stoich_trans
    sto2[:, species:] = stoich_trans
    log_k[...] = jnp.broadcast_to(jnp.log(const_ref[...]) * (2.0 * HALF_LOG2E), (width, reactions)).T

    react_first(edges)
    halo_send(FWD0)
    relay_first(ADJ1, cot, order)
    if inner:
        react_first(inner)

    def advance(s, source, rows):
        for r in rows:
            source[r] = admit[r] * smooth(s, r)
        seed(s, source, rows)

    advance(FWD0, values.at[0], inner)
    halo_wait(FWD0)
    advance(FWD0, values.at[0], edges)
    relay(ADJ1, two, cot, order)
    for r in order:
        field[ADJ1, r] = admit[r] * chosen(ADJ1, r, True)
    halo_send(ADJ1)
    relay_first(FWD0, values.at[0], order)
    for r in inner:
        spread[r] = smooth(ADJ1, r)
    halo_wait(ADJ1)
    for r in edges:
        spread[r] = smooth(ADJ1, r)
    for rows in groups:
        relay(FWD0, two, values.at[0], rows)
    for rows in groups:
        for r in rows:
            state[r] = chosen(FWD0, r, False)
        react_both(rows)
    halo_send(FWD1)
    relay_first(ADJ0, values.at[1], order)
    advance(FWD1, values.at[2], inner)
    halo_wait(FWD1)
    advance(FWD1, values.at[2], edges)
    relay(ADJ0, two, values.at[1], order)
    for r in order:
        field[ADJ0, r] = admit[r] * chosen(ADJ0, r, True)
    halo_send(ADJ0)
    relay_first(FWD1, values.at[2], order)
    for r in inner:
        spread[r] = smooth(ADJ0, r)
    if inner:
        react_last(inner)
    relay(FWD1, two, values.at[2], order)

    def store(source, target, base, r):
        return pltpu.make_async_copy(source.at[r], target.at[:, 0, r, :], out_sem.at[base, r])

    for r in order:
        out_fin[r] = chosen(FWD1, r, False)
        store(out_fin, fin_hbm, 0, r).start()
    for r in inner:
        store(out_adj, adj_hbm, 1, r).start()
    halo_wait(ADJ0)
    for r in edges:
        spread[r] = smooth(ADJ0, r)
    react_last(edges)
    for r in edges:
        store(out_adj, adj_hbm, 1, r).start()

    for s in range(4):
        for d in range(2):
            @pl.when(inside(x + 1 - 2 * d))
            def _():
                for r in range(depth):
                    link(s, d, r).wait_send()

        @pl.when(y > 0)
        def _():
            halo_copies(s)[0].wait_send()

        @pl.when(y < ny - 1)
        def _():
            halo_copies(s)[1].wait_send()
    for r in range(depth):
        store(out_fin, fin_hbm, 0, r).wait()
        store(out_adj, adj_hbm, 1, r).wait()


def solution(mesh):
    sizes = (mesh.shape["gx"], mesh.shape["gy"], mesh.shape["row"])

    def shards(conc, cotangent, courant, direction, rate_const, orders, stoich):
        species, slabs, depth, width = conc.shape
        reactions = orders.shape[0]
        assert slabs == 1
        block = (depth, species, width)
        anywhere = pl.BlockSpec(memory_space=pl.ANY)
        in_hbm = pl.BlockSpec(memory_space=pltpu.HBM)
        vmem = pl.BlockSpec(memory_space=pltpu.VMEM)
        cells = depth * width
        dma = pltpu.SemaphoreType.DMA
        return pl.pallas_call(
            functools.partial(kernel, sizes),
            name="flame_adjoint",
            out_shape=[jax.ShapeDtypeStruct(conc.shape, F32)] * 2,
            in_specs=[in_hbm, in_hbm, vmem, vmem, vmem, in_hbm, in_hbm],
            out_specs=[anywhere, anywhere],
            scratch_shapes=[
                pltpu.VMEM(block, F32), pltpu.VMEM(block, F32), pltpu.VMEM(block, F32), pltpu.VMEM(block, F32),
                pltpu.VMEM((4,) + block, F32), pltpu.VMEM((3,) + block, F32),
                pltpu.VMEM((4, 2) + block, F32), pltpu.VMEM((4, 2) + block, F32), pltpu.VMEM((4, 2) + block[1:], F32),
                pltpu.VMEM(block, F32), pltpu.VMEM(block, F32),
                pltpu.VMEM((reactions, cells), F32), pltpu.VMEM((2, reactions, cells), BF16), pltpu.VMEM((2, reactions, cells), BF16),
                pltpu.VMEM((species, reactions), jnp.int32), pltpu.VMEM((species, reactions), jnp.int32),
                pltpu.VMEM((reactions, 2 * species), BF16), pltpu.VMEM((species, reactions), BF16),
                pltpu.VMEM((reactions, 2 * species), BF16), pltpu.VMEM((species, reactions), BF16),
                pltpu.VMEM((reactions, width), F32),
                dma((2, depth)), dma((2,)), dma((2, depth)),
                dma((4, 2, depth)), dma((4, 2, depth)), dma((4, 2)), dma((4, 2)),
            ],
            compiler_params=pltpu.CompilerParams(collective_id=0, has_side_effects=True, vmem_limit_bytes=67043328),
        )(conc, cotangent, courant, direction, rate_const.reshape(1, reactions), orders.T, stoich)

    placed = (
        P(None, ("grp", "gx"), ("gy", "row"), None),
        P(None, ("grp", "gx"), ("gy", "row"), None),
        P(("grp", "gy", "row"), None),
        P(("grp", "gy", "row"), None),
        P(),
        P(),
        P(),
    )
    return jax.shard_map(
        shards,
        mesh=mesh,
        in_specs=placed,
        out_specs=(P(None, ("grp", "gx"), ("gy", "row"), None),) * 2,
        check_vma=False,
    )
```

time: 121 us -> 41.7 us (0.34)
  starting transfers between devices: 46 us -> 0 us
  Pallas kernels: 0 us -> 38.6 us
  waiting for transfers between devices: 18.3 us -> 0 us
  matrix products: 18.1 us -> 0 us
  other arithmetic: 15.8 us -> 0 us
  blocking collectives: 10.6 us -> 0 us
  local copies, waits for them, and re-layouts: 9.78 us -> 2.26 us
    pallas_call x0 -> x1, Pallas kernels: none -> 38.6 us  [shards(): pl.pallas_call(functools.partial(kernel, sizes), name='flame_adjoint', ou...]
    all_to_all x7 -> x0, starting transfers between devices: 28.7 us -> none  [the longest x3 14.9 us: sweep_fields(): lax.all_to_all(stacked, 'gx', split_axis=1, concat_axis=2, tiled=True)]
    dot_general x8 -> x0, matrix products: 18.1 us -> none  [the longest x2 4.91 us: react_back(): summed = jnp.dot(order_trans, rates * pulled, precision=highest)]
    all_to_all x7 -> x0, waiting for transfers between devices: 17.5 us -> none  [the longest x3 11.7 us: sweep_fields(): lax.all_to_all(stacked, 'gx', split_axis=1, concat_axis=2, tiled=True)]
    ppermute x8 -> x0, starting transfers between devices: 17.3 us -> none  [the longest x4 12.1 us: padded_2(): lax.ppermute(lax.slice_in_dim(block, block.shape[dim] - width, None, axis...]
    all_to_all x1 -> x0, blocking collectives: 10.6 us -> none  [sweep_fields(): lax.all_to_all(stacked, 'gx', split_axis=1, concat_axis=2, tiled=True)]
    pad x16 -> x0, local copies, waits for them, and re-layouts: 6.67 us -> none  [recurrence(): lax.associative_scan(combine_pairs, (multipliers, values), reverse=backwa...]
    another operation x5 -> x0, other arithmetic: 5.66 us -> none  [the longest x4 4.76 us: sweep_fields(): results = jnp.stack([jnp.where(mask, rising, falling)])]
  transfers between devices with their start and end apart: 15 -> 0, of which waited for: 7 -> 0; matrix products, arithmetic and copies ran while one was open for 17% -> 0% of each run, Pallas kernels for 0% -> 0%
where the time goes in v1:
time: 41.7 us; the launch traced here: 41.5 us
  Pallas kernels  38.6 us (93%)
  local copies, waits for them, and re-layouts  2.26 us (5%)
  between operations  0.65 us (2%)
    pallas_call x1, Pallas kernels, shards(): pl.pallas_call(functools.partial(kernel, sizes), name='flame_adjoint', ou...  38.6 us
    unnamed x4, local copies, waits for them, and re-layouts  2.26 us

profile of v1, /device:TPU:0, one launch (start us, length us, event | category | flops | bytes accessed | tf_op | source)
XLA Modules:
  0.0 41.5 jit_solution(1190816727061211645)
XLA Ops:
  0.6 38.6 %flame_adjoint.1 = (f32[64,1,4,128]{3,2,1,0:T(4,128)}, f32[64,1,4,128]{3,2,1,0:T(4,128)}) custom-call(f32[64,1,4,128]{3,2,1,0:T(4,128)} %conc_hbm.1, f32[64,1,4,128]{3,2,1,0:T(4,128)} %cot_hbm.1, f32[4,128]{1,0:T(4,128)} %cour_ref.1, s32[4,128]{1,0:T(4,128)} %dir_ref.1, f32[1,1024]{1,0:T(1,128)} %bitcast.3, s32[64,1024]{1,0:T(8,128)} %bitcast.2, ...), custom_call_target="tpu_custom_call" | custom-call | tf_op jit(solution)/shard_map/flame_adjoint/pallas_call | solution.py:347
  39.3 0.0 copy-start
  39.3 1.6 %copy.11 = f32[64,1,4,128]{3,2,1,0:T(4,128)} copy(f32[64,1,4,128]{3,2,1,0:T(4,128)} %get-tuple-element.4) | data formatting | bytes 262144
  40.9 0.0 copy-done
  40.9 0.7 %copy.12 = f32[64,1,4,128]{3,2,1,0:T(4,128)} copy(f32[64,1,4,128]{3,2,1,0:T(4,128)S(1)} %copy-done) | data formatting | bytes 262144
Async XLA Ops:
  39.3 1.6 %copy-start = (f32[64,1,4,128]{3,2,1,0:T(4,128)S(1)}, f32[64,1,4,128]{3,2,1,0:T(4,128)}, u32[]{:S(2)}) copy-start(f32[64,1,4,128]{3,2,1,0:T(4,128)} %get-tuple-element.5) | copy-start | bytes 393220

commit v2 on v1

v2 whole, which is shorter than its diff:
```python
import functools

import jax
import jax.numpy as jnp
from jax import lax
from jax.experimental import pallas as pl
from jax.experimental.pallas import tpu as pltpu
from jax.sharding import PartitionSpec as P

MESH = pl.DeviceIdType.MESH
F32 = jnp.float32
BF16 = jnp.bfloat16
TIME_STEP = 0.1
DIFFUSION = 0.1
HALF_LOG2E = 0.5 * 1.4426950408889634
FWD0, ADJ1, FWD1, ADJ0 = range(4)


def kernel(
    sizes, conc_hbm, cot_hbm, cour_ref, dir_ref, const_ref, ord_hbm, sto_hbm, out_fin, out_adj,
    conc, cot, state, spread, field, values, recv, sent, halo, star, rates0, rates_b, grad_b,
    ord_i, sto_i, ord2, ord_t, sto2, sto, log_k,
    in_sem, tab_sem, send_sem, recv_sem, hsend_sem, hrecv_sem,
):
    nx, ngy, nrow = sizes
    ny = ngy * nrow
    depth, species, width = conc.shape
    reactions = ord_i.shape[1]
    edges = sorted({0, depth - 1})
    inner = list(range(1, depth - 1))
    groups = [g for g in (edges, inner) if g]
    order = [r for g in groups for r in g]
    chunk = min(256, reactions)
    pieces = send_sem.shape[3]
    piece = species // pieces

    x = lax.axis_index("gx")
    y = lax.axis_index("gy") * nrow + lax.axis_index("row")

    def line(target):
        return {"gy": lax.div(target, nrow), "row": lax.rem(target, nrow)}

    neighbours = [
        (x > 0, {"gx": x - 1}), (x < nx - 1, {"gx": x + 1}),
        (y > 0, line(y - 1)), (y < ny - 1, line(y + 1)),
    ]

    def load(item):
        source, target, base = item
        return [pltpu.make_async_copy(source.at[:, 0, r, :], target.at[r], in_sem.at[base, r]) for r in range(depth)]

    loads_cot = load((cot_hbm, cot, 0))
    loads_conc = load((conc_hbm, conc, 1))
    tables = [pltpu.make_async_copy(ord_hbm, ord_i, tab_sem.at[0]), pltpu.make_async_copy(sto_hbm, sto_i, tab_sem.at[1])]
    for copy in tables + loads_conc + loads_cot:
        copy.start()

    barrier = pltpu.get_barrier_semaphore()
    for there, device in neighbours:
        @pl.when(there)
        def _():
            pl.semaphore_signal(barrier, inc=1, device_id=device, device_id_type=MESH)

    @pl.when(x == 0)
    def _():
        for s in range(4):
            recv[s, 0] = jnp.zeros_like(recv[s, 0])

    @pl.when(x == nx - 1)
    def _():
        for s in range(4):
            recv[s, 1] = jnp.zeros_like(recv[s, 1])

    @pl.when(y == 0)
    def _():
        for s in range(4):
            halo[s, 0] = jnp.zeros_like(halo[s, 0])

    @pl.when(y == ny - 1)
    def _():
        for s in range(4):
            halo[s, 1] = jnp.zeros_like(halo[s, 1])

    courant = cour_ref[...]
    retain_all = courant / (1.0 + courant)
    admit_all = 1.0 / (1.0 + courant)
    retain = [retain_all[r:r + 1] for r in range(depth)]
    admit = [admit_all[r:r + 1] for r in range(depth)]
    rising = [jnp.broadcast_to(dir_ref[r:r + 1], (species, width)) for r in range(depth)]

    for copy in tables:
        copy.wait()
    order_float = ord_i[...].astype(F32)
    ord_t[...] = order_float.astype(BF16)
    order_trans = order_float.T.astype(BF16)
    ord2[:, :species] = order_trans
    ord2[:, species:] = order_trans
    stoich_float = sto_i[...].astype(F32)
    sto[...] = stoich_float.astype(BF16)
    stoich_trans = stoich_float.T.astype(BF16)
    sto2[:, :species] = stoich_trans
    sto2[:, species:] = stoich_trans
    log_k[...] = jnp.broadcast_to(jnp.log(const_ref[...]) * (2.0 * HALF_LOG2E), (width, reactions)).T
    for copy in loads_conc + loads_cot:
        copy.wait()
    pl.semaphore_wait(barrier, sum(jnp.where(there, 1, 0) for there, _ in neighbours))

    one = jnp.where(x < (nx + 1) // 2, 0, 1)
    two = 1 - one

    def link(s, d, r, h):
        part = pl.ds(h * piece, piece)
        return pltpu.make_async_remote_copy(
            src_ref=sent.at[s, d, r, part], dst_ref=recv.at[s, d, r, part],
            send_sem=send_sem.at[s, d, r, h], recv_sem=recv_sem.at[s, d, r, h],
            device_id={"gx": x + 1 - 2 * d}, device_id_type=MESH,
        )

    def inside(position):
        return (position >= 0) & (position < nx)

    def relay(s, d, source, rows, arrive=True):
        pred, succ = inside(x - 1 + 2 * d), inside(x + 1 - 2 * d)
        for r in rows:
            for h in range(pieces):
                part = pl.ds(h * piece, piece)
                if arrive:
                    @pl.when(pred)
                    def _():
                        link(s, d, r, h).wait_recv()
                sent[s, d, r, part] = source[r, part] + retain[r] * recv[s, d, r, part]

                @pl.when(succ)
                def _():
                    link(s, d, r, h).start()

    first_end = jnp.logical_not(inside(x - 1 + 2 * one))

    def seed(s, source, rows):
        @pl.when(first_end)
        def _():
            relay(s, one, source, rows, arrive=False)

    def relay_first(s, source, rows):
        @pl.when(jnp.logical_not(first_end))
        def _():
            relay(s, one, source, rows)

    def chosen(s, r, adjoint):
        pick = (rising[r] == 0) if adjoint else (rising[r] == 1)
        return jnp.where(pick, sent[s, 0, r], sent[s, 1, r])

    def halo_copies(s):
        source = conc if s == FWD0 else field.at[s]
        down = pltpu.make_async_remote_copy(
            src_ref=source.at[0], dst_ref=halo.at[s, 1], send_sem=hsend_sem.at[s, 0], recv_sem=hrecv_sem.at[s, 1],
            device_id=line(y - 1), device_id_type=MESH)
        up = pltpu.make_async_remote_copy(
            src_ref=source.at[depth - 1], dst_ref=halo.at[s, 0], send_sem=hsend_sem.at[s, 1], recv_sem=hrecv_sem.at[s, 0],
            device_id=line(y + 1), device_id_type=MESH)
        return down, up

    def halo_send(s):
        @pl.when(y > 0)
        def _():
            halo_copies(s)[0].start()

        @pl.when(y < ny - 1)
        def _():
            halo_copies(s)[1].start()

    def halo_wait(s):
        @pl.when(y > 0)
        def _():
            halo_copies(s)[1].wait_recv()

        @pl.when(y < ny - 1)
        def _():
            halo_copies(s)[0].wait_recv()

    lane = lax.broadcasted_iota(jnp.int32, (species, width), 1)

    def smooth(s, r):
        here = field[s, r]
        ends = star if s == FWD0 else halo.at[s]
        below = ends[0] if r == 0 else field[s, r - 1]
        above = ends[1] if r == depth - 1 else field[s, r + 1]
        before = jnp.where(lane == 0, 0.0, pltpu.roll(here, 1, 1))
        after = jnp.where(lane == width - 1, 0.0, pltpu.roll(here, width - 1, 1))
        return here + DIFFUSION * (above + below + after + before - 4.0 * here)

    def side(parts):
        return parts[0] if len(parts) == 1 else jnp.concatenate(parts, axis=1)

    def split(value):
        high = value.astype(BF16)
        low = (value - high.astype(F32)).astype(BF16)
        return jnp.concatenate([high, low], axis=0)

    def activity(rows, source):
        return split(side([HALF_LOG2E * jnp.log(1.0 + source[r] * source[r]) for r in rows]))

    def rates_at(part, act, count):
        exponent = jnp.dot(ord2[part, :], act, preferred_element_type=F32)
        return jnp.exp2(exponent + side([log_k[part, :]] * count))

    parts = [pl.ds(i, chunk) for i in range(0, reactions, chunk)]

    def keep(target, part, cols, value):
        high = value.astype(BF16)
        target[0, part, cols] = high
        target[1, part, cols] = (value - high.astype(F32)).astype(BF16)

    def gather(table, halves, cols):
        small = jnp.dot(table[...], halves[1, :, cols], preferred_element_type=F32)
        return small + jnp.dot(table[...], halves[0, :, cols], preferred_element_type=F32)

    def columns(rows):
        start = order.index(rows[0]) * width
        return pl.ds(start, len(rows) * width)

    def put_react(rows, source, s, produced):
        for i, r in enumerate(rows):
            field[s, r] = source[r] + TIME_STEP * produced[:, i * width:(i + 1) * width]

    def react_first(rows):
        act, cols = activity(rows, conc), columns(rows)
        for part in parts:
            rates = rates_at(part, act, len(rows))
            rates0[part, cols] = rates
            keep(rates_b, part, cols, rates)
        put_react(rows, conc, FWD0, gather(sto, rates_b, cols))

    def react_halo():
        act, cols = activity([0, 1], halo.at[FWD0]), pl.ds(0, 2 * width)
        for part in parts:
            keep(rates_b, part, cols, rates_at(part, act, 2))
        produced = gather(sto, rates_b, cols)
        for i, there in enumerate((y > 0, y < ny - 1)):
            value = halo[FWD0, i] + TIME_STEP * produced[:, i * width:(i + 1) * width]
            star[i] = jnp.where(there, value, 0.0)

    def put_back(rows, cells, summed, target):
        for i, r in enumerate(rows):
            c = cells[r]
            target[r] = spread[r] + TIME_STEP * c / (1.0 + c * c) * summed[:, i * width:(i + 1) * width]

    def react_both(rows):
        act, cols = activity(rows, state), columns(rows)
        push = split(side([spread[r] for r in rows]))
        for part in parts:
            rates = rates_at(part, act, len(rows))
            pulled = jnp.dot(sto2[part, :], push, preferred_element_type=F32)
            keep(rates_b, part, cols, rates)
            keep(grad_b, part, cols, rates * pulled)
        put_back(rows, state, gather(ord_t, grad_b, cols), values.at[1])
        seed(ADJ0, values.at[1], rows)
        put_react(rows, state, FWD1, gather(sto, rates_b, cols))

    def react_last(rows):
        cols = columns(rows)
        push = split(side([spread[r] for r in rows]))
        for part in parts:
            pulled = jnp.dot(sto2[part, :], push, preferred_element_type=F32)
            keep(grad_b, part, cols, rates0[part, cols] * pulled)
        put_back(rows, conc, gather(ord_t, grad_b, cols), out_adj)

    def advance(s, source, rows):
        for r in rows:
            source[r] = admit[r] * smooth(s, r)
        seed(s, source, rows)

    def arrive_back(s, source):
        for rows in groups:
            relay(s, two, source, rows)
            for r in rows:
                field[s, r] = admit[r] * chosen(s, r, True)
            if rows is groups[0]:
                halo_send(s)

    halo_send(FWD0)
    seed(ADJ1, cot, order)
    for rows in groups:
        react_first(rows)
    relay_first(ADJ1, cot, order)
    halo_wait(FWD0)
    react_halo()
    advance(FWD0, values.at[0], edges)
    advance(FWD0, values.at[0], inner)
    arrive_back(ADJ1, cot)
    relay_first(FWD0, values.at[0], order)
    for r in inner:
        spread[r] = smooth(ADJ1, r)
    halo_wait(ADJ1)
    for r in edges:
        spread[r] = smooth(ADJ1, r)
    for rows in groups:
        relay(FWD0, two, values.at[0], rows)
        for r in rows:
            state[r] = chosen(FWD0, r, False)
        react_both(rows)
        if rows is groups[0]:
            halo_send(FWD1)
    relay_first(ADJ0, values.at[1], order)
    advance(FWD1, values.at[2], inner)
    halo_wait(FWD1)
    advance(FWD1, values.at[2], edges)
    arrive_back(ADJ0, values.at[1])
    relay_first(FWD1, values.at[2], inner + edges)
    for r in inner:
        spread[r] = smooth(ADJ0, r)
    if inner:
        react_last(inner)
    relay(FWD1, two, values.at[2], inner + edges)
    for r in order:
        out_fin[r] = chosen(FWD1, r, False)
    halo_wait(ADJ0)
    for r in edges:
        spread[r] = smooth(ADJ0, r)
    react_last(edges)

    for s in range(4):
        for d in range(2):
            @pl.when(inside(x + 1 - 2 * d))
            def _():
                for r in range(depth):
                    for h in range(pieces):
                        link(s, d, r, h).wait_send()

        @pl.when(y > 0)
        def _():
            halo_copies(s)[0].wait_send()

        @pl.when(y < ny - 1)
        def _():
            halo_copies(s)[1].wait_send()


def solution(mesh):
    sizes = (mesh.shape["gx"], mesh.shape["gy"], mesh.shape["row"])

    def shards(conc, cotangent, courant, direction, rate_const, orders, stoich):
        species, slabs, depth, width = conc.shape
        reactions = orders.shape[0]
        assert slabs == 1
        block = (depth, species, width)
        in_hbm = pl.BlockSpec(memory_space=pltpu.HBM)
        vmem = pl.BlockSpec(memory_space=pltpu.VMEM)
        cells = depth * width
        dma = pltpu.SemaphoreType.DMA
        pieces = 2 if species % 16 == 0 else 1
        outs = pl.pallas_call(
            functools.partial(kernel, sizes),
            name="flame_adjoint",
            out_shape=[jax.ShapeDtypeStruct(block, F32)] * 2,
            in_specs=[in_hbm, in_hbm, vmem, vmem, vmem, in_hbm, in_hbm],
            out_specs=[vmem, vmem],
            scratch_shapes=[
                pltpu.VMEM(block, F32), pltpu.VMEM(block, F32), pltpu.VMEM(block, F32), pltpu.VMEM(block, F32),
                pltpu.VMEM((4,) + block, F32), pltpu.VMEM((3,) + block, F32),
                pltpu.VMEM((4, 2) + block, F32), pltpu.VMEM((4, 2) + block, F32), pltpu.VMEM((4, 2) + block[1:], F32),
                pltpu.VMEM((2,) + block[1:], F32),
                pltpu.VMEM((reactions, cells), F32), pltpu.VMEM((2, reactions, cells), BF16), pltpu.VMEM((2, reactions, cells), BF16),
                pltpu.VMEM((species, reactions), jnp.int32), pltpu.VMEM((species, reactions), jnp.int32),
                pltpu.VMEM((reactions, 2 * species), BF16), pltpu.VMEM((species, reactions), BF16),
                pltpu.VMEM((reactions, 2 * species), BF16), pltpu.VMEM((species, reactions), BF16),
                pltpu.VMEM((reactions, width), F32),
                dma((2, depth)), dma((2,)),
                dma((4, 2, depth, pieces)), dma((4, 2, depth, pieces)), dma((4, 2)), dma((4, 2)),
            ],
            compiler_params=pltpu.CompilerParams(collective_id=0, has_side_effects=True, vmem_limit_bytes=67043328),
        )(conc, cotangent, courant, direction, rate_const.reshape(1, reactions), orders.T, stoich)
        return tuple(out.transpose(1, 0, 2)[:, None] for out in outs)

    placed = (
        P(None, ("grp", "gx"), ("gy", "row"), None),
        P(None, ("grp", "gx"), ("gy", "row"), None),
        P(("grp", "gy", "row"), None),
        P(("grp", "gy", "row"), None),
        P(),
        P(),
        P(),
    )
    return jax.shard_map(
        shards,
        mesh=mesh,
        in_specs=placed,
        out_specs=(P(None, ("grp", "gx"), ("gy", "row"), None),) * 2,
        check_vma=False,
    )
```

time: 41.7 us -> 40.9 us (0.981)
  Pallas kernels: 38.6 us -> 37.6 us
    pallas_call x1, Pallas kernels: 38.6 us -> 37.6 us  [shards(): pl.pallas_call(functools.partial(kernel, sizes), name='flame_adjoint', ou...]
where the time goes in v2:
time: 40.9 us; the launch traced here: 40.7 us
  Pallas kernels  37.6 us (92%)
  local copies, waits for them, and re-layouts  2.43 us (6%)
  between operations  0.65 us (2%)
    pallas_call x1, Pallas kernels, shards(): pl.pallas_call(functools.partial(kernel, sizes), name='flame_adjoint', ou...  37.6 us
    unnamed x4, local copies, waits for them, and re-layouts  2.43 us

profile of v2, /device:TPU:0, one launch (start us, length us, event | category | flops | bytes accessed | tf_op | source)
XLA Modules:
  0.0 40.7 jit_solution(16947700195785326756)
XLA Ops:
  0.6 37.6 %flame_adjoint.1 = (f32[4,64,128]{2,1,0:T(8,128)}, f32[4,64,128]{2,1,0:T(8,128)}) custom-call(f32[64,1,4,128]{3,2,1,0:T(4,128)} %conc_hbm.1, f32[64,1,4,128]{3,2,1,0:T(4,128)} %cot_hbm.1, f32[4,128]{1,0:T(4,128)} %cour_ref.1, s32[4,128]{1,0:T(4,128)} %dir_ref.1, f32[1,1024]{1,0:T(1,128)} %bitcast.11, s32[64,1024]{1,0:T(8,128)} %bitcast.8, s32[64,1024]{1,0:T(8,128)} %sto_hbm.1), custom_call_target="tpu_custom_call" | custom-call | tf_op jit(solution)/shard_map/flame_adjoint/pallas_call | solution.py:352
  38.2 0.0 copy-start
  38.2 1.7 %copy.9 = f32[64,1,4,128]{3,2,1,0:T(4,128)} copy(f32[64,1,4,128]{3,0,2,1:T(8,128)} %bitcast.10) | data formatting | bytes 262144
  39.9 0.0 copy-done
  39.9 0.7 %copy.10 = f32[64,1,4,128]{3,2,1,0:T(4,128)} copy(f32[64,1,4,128]{3,0,2,1:T(8,128)S(1)} %bitcast.9) | data formatting | bytes 262144
Async XLA Ops:
  38.2 1.7 %copy-start = (f32[4,64,128]{2,1,0:T(8,128)S(1)}, f32[4,64,128]{2,1,0:T(8,128)}, u32[]{:S(2)}) copy-start(f32[4,64,128]{2,1,0:T(8,128)} %get-tuple-element.5) | copy-start | bytes 393220

commit v3 on v2

--- a/solution.py
+++ b/solution.py
@@ -255,7 +255,8 @@
             keep(grad_b, part, cols, rates * pulled)
         put_back(rows, state, gather(ord_t, grad_b, cols), values.at[1])
         seed(ADJ0, values.at[1], rows)
-        put_react(rows, state, FWD1, gather(sto, rates_b, cols))
+    def react_next(rows):
+        put_react(rows, state, FWD1, gather(sto, rates_b, columns(rows)))
 
     def react_last(rows):
         cols = columns(rows)
@@ -299,6 +300,8 @@
         for r in rows:
             state[r] = chosen(FWD0, r, False)
         react_both(rows)
+    for rows in groups:
+        react_next(rows)
         if rows is groups[0]:
             halo_send(FWD1)
     relay_first(ADJ0, values.at[1], order)
@@ -368,8 +371,8 @@
                 dma((2, depth)), dma((2,)),
                 dma((4, 2, depth, pieces)), dma((4, 2, depth, pieces)), dma((4, 2)), dma((4, 2)),
             ],
-            compiler_params=pltpu.CompilerParams(collective_id=0, has_side_effects=True, vmem_limit_bytes=67043328),
-        )(conc, cotangent, courant, direction, rate_const.reshape(1, reactions), orders.T, stoich)
+            compiler_params=pltpu.CompilerParams(collective_id=0, has_side_effects=True, vmem_limit_bytes=48 * 1024 * 1024),
+        )(*[pltpu.with_memory_space_constraint(a, pltpu.HBM) for a in (conc, cotangent, courant, direction, rate_const.reshape(1, reactions), orders.T, stoich)])
         return tuple(out.transpose(1, 0, 2)[:, None] for out in outs)
 
     placed = (

time: 40.9 us -> 39.1 us (0.956)
  local copies, waits for them, and re-layouts: 2.43 us -> 1.48 us
  Pallas kernels: 37.6 us -> 36.8 us
    unnamed x4 -> x2, local copies, waits for them, and re-layouts: 2.43 us -> 1.48 us
    pallas_call x1, Pallas kernels: 37.6 us -> 36.8 us  [shards(): pl.pallas_call(functools.partial(kernel, sizes), name='flame_adjoint', ou...]
where the time goes in v3:
time: 39.1 us; the launch traced here: 38.9 us
  Pallas kernels  36.8 us (94%)
  local copies, waits for them, and re-layouts  1.48 us (4%)
  between operations  0.64 us (2%)
    pallas_call x1, Pallas kernels, shards(): pl.pallas_call(functools.partial(kernel, sizes), name='flame_adjoint', ou...  36.8 us
    unnamed x2, local copies, waits for them, and re-layouts  1.48 us

profile of v3, /device:TPU:0, one launch (start us, length us, event | category | flops | bytes accessed | tf_op | source)
XLA Modules:
  0.0 38.9 jit_solution(7250649425183346228)
XLA Ops:
  0.6 36.8 %flame_adjoint.1 = (f32[4,64,128]{2,1,0:T(8,128)S(1)}, f32[4,64,128]{2,1,0:T(8,128)S(1)}) custom-call(f32[64,1,4,128]{3,2,1,0:T(4,128)} %conc_hbm.1, f32[64,1,4,128]{3,2,1,0:T(4,128)} %cot_hbm.1, f32[4,128]{1,0:T(4,128)} %cour_ref.1, s32[4,128]{1,0:T(4,128)} %dir_ref.1, f32[1,1024]{1,0:T(1,128)} %bitcast.11, s32[64,1024]{1,0:T(8,128)} %bitcast.10, ...), custom_call_target="tpu_custom_call" | custom-call | tf_op jit(solution)/shard_map/flame_adjoint/pallas_call | solution.py:355
  37.4 0.7 %copy.9 = f32[64,1,4,128]{3,2,1,0:T(4,128)} copy(f32[64,1,4,128]{3,0,2,1:T(8,128)S(1)} %bitcast.9) | data formatting | bytes 262144
  38.1 0.7 %copy.10 = f32[64,1,4,128]{3,2,1,0:T(4,128)} copy(f32[64,1,4,128]{3,0,2,1:T(8,128)S(1)} %bitcast.8) | data formatting | bytes 262144
